TPU v7x, 32 devices: a whole 2x2x4 slice. The times are simulated.
32 devices in a mesh: row: 8 (over z, core), col: 4 (over y, x).
Axes of the slice: x: 2, y: 2, z: 4, core: 2. Of those that a mesh axis runs over, the one named last changes fastest.
Arguments:
- pivot_inverse: float32 [1024, 1024], P('row'), may hold values from -1 to 2, as said below
- panel: float32 [16, 1024, 1024], P('row', 'col'), may hold values from -1 to 1
- trailing: float32 [160, 1024, 1024], P('row', None, 'col'), may hold values from -6 to 6
- tile_list: int32 [160, 2], P('row'), may hold values from -1 to 15, as said below
Outputs:
- solved_panel: float32 [16, 1024, 1024], P('row', 'col')
- updated: float32 [160, 1024, 1024], P('row', None, 'col')
Inputs may be any that keep to these rules, and one draw needn't show every extreme that they name: `pivot_inverse`: lower triangular, diagonal between 0.5 and 2. `tile_list`: slots t of group g are g * 20 to g * 20 + 19. Column 0 lies in 0 to 1; column 1 is a panel tile or -1 for an empty slot. The live slots of a group come first and name distinct pairs; each group in the first half of the groups holds exactly 6 live slots, each in the second half exactly 20. Empty slots hold 0 in column 0.
All inputs are finite; a program needn't handle non-finite values.
Results may differ from a plain program's by a relative error of at most 0.00007.
Values sent between devices are 32-bit elements; how exact they have to be, the bound alone decides.
A program may use at most 128 MiB of HBM per device.

v0:
```python
import jax
import jax.numpy as jnp
from jax import lax
from jax.sharding import PartitionSpec as P

highest = lax.Precision.HIGHEST


def slot_term(left_tile, right_rows):
    return jnp.einsum("ak,bk->ab", left_tile, right_rows, precision=highest)


def per_device(pivot_inverse, panel, trailing, tile_list):
    full_pivot = lax.all_gather(pivot_inverse, "row", axis=0, tiled=True)
    slice_rows = panel.shape[1]
    tile_order = panel.shape[2]
    solved = jnp.einsum("pak,jk->paj", panel, full_pivot, precision=highest)
    whole_tiles = lax.all_gather(solved, "col", axis=1, tiled=True)
    slices = lax.all_gather(solved, "row", axis=0, tiled=True)
    empty_term = jnp.zeros((tile_order, slice_rows), jnp.float32)

    def owner_slot(listed):
        return lax.cond(
            listed[1] >= 0,
            lambda: slot_term(whole_tiles[listed[0]], slices[jnp.maximum(listed[1], 0)]),
            lambda: empty_term,
        )

    updates = lax.map(owner_slot, tile_list)
    return (solved, trailing - updates)


def solution(mesh):
    placed = (P("row", None), P("row", "col", None), P("row", None, "col"), P("row", None))
    return jax.shard_map(
        per_device,
        mesh=mesh,
        in_specs=placed,
        out_specs=(P("row", "col", None), P("row", None, "col")),
        check_vma=False,
    )
```

profile of v0, /device:TPU:17, one launch (start us, length us, event | category | flops | bytes accessed | tf_op | source)
XLA Modules:
  0.0 549.2 jit_solution(17229575436404876348)
XLA Ops:
  8.0 48.8 %all-gather.4.cloned.1.call-done = f32[1024,1024]{1,0:T(8,128)} async-done(((f32[128,1024]{1,0:T(8,128)}), f32[1024,1024]{1,0:T(8,128)}) %all-gather.4.cloned.1.call-update) | async-done | bytes 4194320 | tf_op jit(solution)/shard_map/all_gather | solution.py:14
  56.8 9.6 %fusion.9 = f32[2,256,1024]{2,1,0:T(8,128)} fusion(f32[2,256,1024]{2,1,0:T(8,128)S(1)} %copy-done, f32[1024,1024]{1,0:T(8,128)} %all-gather.4.cloned.1.call-done), kind=kOutput, calls=%fused_computation.9 | convolution fusion | flops 6442450944 | bytes 8388608 | tf_op jit(solution)/shard_map/pak,jk->paj/dot_general | solution.py:17
  67.3 86.2 %all-gather.6.cloned.1.call-done = f32[2,1024,1024]{2,1,0:T(8,128)} async-done(((f32[2,256,1024]{2,1,0:T(8,128)}), f32[2,1024,1024]{2,1,0:T(8,128)}) %all-gather.6.cloned.1.call-update) | async-done | bytes 8388624 | tf_op jit(solution)/shard_map/all_gather | solution.py:18
  153.5 152.1 %all-gather.8.cloned.1.call-done = f32[16,256,1024]{2,1,0:T(8,128)} async-done(((f32[2,256,1024]{2,1,0:T(8,128)}), f32[16,256,1024]{2,1,0:T(8,128)}) %all-gather.8.cloned.1.call-update) | async-done | bytes 16777232 | tf_op jit(solution)/shard_map/all_gather | solution.py:19
  305.6 215.2 %while.10 = (s32[]{:T(128)}, f32[20,1024,256]{2,1,0:T(8,128)}, s32[20,2]{1,0:T(8,128)S(1)}, f32[2,1024,1024]{2,1,0:T(8,128)}, f32[16,256,1024]{2,1,0:T(8,128)}, /*index=5*/s32[]{:T(128)}, s32[1,1]{1,0:T(1,128)}) while((s32[]{:T(128)}, f32[20,1024,256]{2,1,0:T(8,128)}, s32[20,2]{1,0:T(8,128)S(1)}, f32[2,1024,1024]{2,1,0:T(8,128)}, ...), condition=%wide.region_3.4_spmd, body=%wide.region_0.3_spmd.sunk | while | flops 3221225472 | bytes 8389849 | solution.py:29
  306.7 8.5 %conditional.2 = (f32[1,1024,256]{2,1,0:T(8,128)S(1)}) conditional(s32[]{:T(128)} %bitcast.18, () %tuple.35, (s32[1,2]{1,0:T(1,128)S(1)}, f32[2,1024,1024]{2,1,0:T(8,128)}, f32[16,256,1024]{2,1,0:T(8,128)}) %tuple.36), branch_computations={%region_1.1_spmd, %region_2.2_spmd} | conditional | flops 3221225472 | bytes 6292042 | solution.py:23
  317.5 8.5 %conditional.2 = (f32[1,1024,256]{2,1,0:T(8,128)S(1)}) conditional(s32[]{:T(128)} %bitcast.18, () %tuple.35, (s32[1,2]{1,0:T(1,128)S(1)}, f32[2,1024,1024]{2,1,0:T(8,128)}, f32[16,256,1024]{2,1,0:T(8,128)}) %tuple.36), branch_computations={%region_1.1_spmd, %region_2.2_spmd} | conditional | flops 3221225472 | bytes 6292042 | solution.py:23
  328.2 8.6 %conditional.2 = (f32[1,1024,256]{2,1,0:T(8,128)S(1)}) conditional(s32[]{:T(128)} %bitcast.18, () %tuple.35, (s32[1,2]{1,0:T(1,128)S(1)}, f32[2,1024,1024]{2,1,0:T(8,128)}, f32[16,256,1024]{2,1,0:T(8,128)}) %tuple.36), branch_computations={%region_1.1_spmd, %region_2.2_spmd} | conditional | flops 3221225472 | bytes 6292042 | solution.py:23
  331.2 5.6 %fusion.3 = f32[1,1024,256]{2,1,0:T(8,128)S(1)} fusion(f32[2,1024,1024]{2,1,0:T(8,128)} %get-tuple-element.31, s32[]{:T(128)S(6)} %select_n.0, f32[16,256,1024]{2,1,0:T(8,128)} %get-tuple-element.33, s32[]{:T(128)} %bitcast.2), kind=kOutput, calls=%fused_computation.3 | convolution fusion | flops 3221225472 | bytes 6291972 | tf_op jit(solution)/shard_map/while/body/eval_jaxpr/cond/branch_1_fun/ak,bk->ab/dot_general | solution.py:10
  339.0 8.5 %conditional.2 = (f32[1,1024,256]{2,1,0:T(8,128)S(1)}) conditional(s32[]{:T(128)} %bitcast.18, () %tuple.35, (s32[1,2]{1,0:T(1,128)S(1)}, f32[2,1024,1024]{2,1,0:T(8,128)}, f32[16,256,1024]{2,1,0:T(8,128)}) %tuple.36), branch_computations={%region_1.1_spmd, %region_2.2_spmd} | conditional | flops 3221225472 | bytes 6292042 | solution.py:23
  349.8 8.6 %conditional.2 = (f32[1,1024,256]{2,1,0:T(8,128)S(1)}) conditional(s32[]{:T(128)} %bitcast.18, () %tuple.35, (s32[1,2]{1,0:T(1,128)S(1)}, f32[2,1024,1024]{2,1,0:T(8,128)}, f32[16,256,1024]{2,1,0:T(8,128)}) %tuple.36), branch_computations={%region_1.1_spmd, %region_2.2_spmd} | conditional | flops 3221225472 | bytes 6292042 | solution.py:23
  352.7 5.6 %fusion.3 = f32[1,1024,256]{2,1,0:T(8,128)S(1)} fusion(f32[2,1024,1024]{2,1,0:T(8,128)} %get-tuple-element.31, s32[]{:T(128)S(6)} %select_n.0, f32[16,256,1024]{2,1,0:T(8,128)} %get-tuple-element.33, s32[]{:T(128)} %bitcast.2), kind=kOutput, calls=%fused_computation.3 | convolution fusion | flops 3221225472 | bytes 6291972 | tf_op jit(solution)/shard_map/while/body/eval_jaxpr/cond/branch_1_fun/ak,bk->ab/dot_general | solution.py:10
  360.5 8.5 %conditional.2 = (f32[1,1024,256]{2,1,0:T(8,128)S(1)}) conditional(s32[]{:T(128)} %bitcast.18, () %tuple.35, (s32[1,2]{1,0:T(1,128)S(1)}, f32[2,1024,1024]{2,1,0:T(8,128)}, f32[16,256,1024]{2,1,0:T(8,128)}) %tuple.36), branch_computations={%region_1.1_spmd, %region_2.2_spmd} | conditional | flops 3221225472 | bytes 6292042 | solution.py:23
  371.3 8.6 %conditional.2 = (f32[1,1024,256]{2,1,0:T(8,128)S(1)}) conditional(s32[]{:T(128)} %bitcast.18, () %tuple.35, (s32[1,2]{1,0:T(1,128)S(1)}, f32[2,1024,1024]{2,1,0:T(8,128)}, f32[16,256,1024]{2,1,0:T(8,128)}) %tuple.36), branch_computations={%region_1.1_spmd, %region_2.2_spmd} | conditional | flops 3221225472 | bytes 6292042 | solution.py:23
  374.2 5.6 %fusion.3 = f32[1,1024,256]{2,1,0:T(8,128)S(1)} fusion(f32[2,1024,1024]{2,1,0:T(8,128)} %get-tuple-element.31, s32[]{:T(128)S(6)} %select_n.0, f32[16,256,1024]{2,1,0:T(8,128)} %get-tuple-element.33, s32[]{:T(128)} %bitcast.2), kind=kOutput, calls=%fused_computation.3 | convolution fusion | flops 3221225472 | bytes 6291972 | tf_op jit(solution)/shard_map/while/body/eval_jaxpr/cond/branch_1_fun/ak,bk->ab/dot_general | solution.py:10
  382.0 8.5 %conditional.2 = (f32[1,1024,256]{2,1,0:T(8,128)S(1)}) conditional(s32[]{:T(128)} %bitcast.18, () %tuple.35, (s32[1,2]{1,0:T(1,128)S(1)}, f32[2,1024,1024]{2,1,0:T(8,128)}, f32[16,256,1024]{2,1,0:T(8,128)}) %tuple.36), branch_computations={%region_1.1_spmd, %region_2.2_spmd} | conditional | flops 3221225472 | bytes 6292042 | solution.py:23
  392.8 8.6 %conditional.2 = (f32[1,1024,256]{2,1,0:T(8,128)S(1)}) conditional(s32[]{:T(128)} %bitcast.18, () %tuple.35, (s32[1,2]{1,0:T(1,128)S(1)}, f32[2,1024,1024]{2,1,0:T(8,128)}, f32[16,256,1024]{2,1,0:T(8,128)}) %tuple.36), branch_computations={%region_1.1_spmd, %region_2.2_spmd} | conditional | flops 3221225472 | bytes 6292042 | solution.py:23
  403.6 8.5 %conditional.2 = (f32[1,1024,256]{2,1,0:T(8,128)S(1)}) conditional(s32[]{:T(128)} %bitcast.18, () %tuple.35, (s32[1,2]{1,0:T(1,128)S(1)}, f32[2,1024,1024]{2,1,0:T(8,128)}, f32[16,256,1024]{2,1,0:T(8,128)}) %tuple.36), branch_computations={%region_1.1_spmd, %region_2.2_spmd} | conditional | flops 3221225472 | bytes 6292042 | solution.py:23
  414.3 8.6 %conditional.2 = (f32[1,1024,256]{2,1,0:T(8,128)S(1)}) conditional(s32[]{:T(128)} %bitcast.18, () %tuple.35, (s32[1,2]{1,0:T(1,128)S(1)}, f32[2,1024,1024]{2,1,0:T(8,128)}, f32[16,256,1024]{2,1,0:T(8,128)}) %tuple.36), branch_computations={%region_1.1_spmd, %region_2.2_spmd} | conditional | flops 3221225472 | bytes 6292042 | solution.py:23
  417.3 5.6 %fusion.3 = f32[1,1024,256]{2,1,0:T(8,128)S(1)} fusion(f32[2,1024,1024]{2,1,0:T(8,128)} %get-tuple-element.31, s32[]{:T(128)S(6)} %select_n.0, f32[16,256,1024]{2,1,0:T(8,128)} %get-tuple-element.33, s32[]{:T(128)} %bitcast.2), kind=kOutput, calls=%fused_computation.3 | convolution fusion | flops 3221225472 | bytes 6291972 | tf_op jit(solution)/shard_map/while/body/eval_jaxpr/cond/branch_1_fun/ak,bk->ab/dot_general | solution.py:10
  425.1 8.5 %conditional.2 = (f32[1,1024,256]{2,1,0:T(8,128)S(1)}) conditional(s32[]{:T(128)} %bitcast.18, () %tuple.35, (s32[1,2]{1,0:T(1,128)S(1)}, f32[2,1024,1024]{2,1,0:T(8,128)}, f32[16,256,1024]{2,1,0:T(8,128)}) %tuple.36), branch_computations={%region_1.1_spmd, %region_2.2_spmd} | conditional | flops 3221225472 | bytes 6292042 | solution.py:23
  435.8 8.6 %conditional.2 = (f32[1,1024,256]{2,1,0:T(8,128)S(1)}) conditional(s32[]{:T(128)} %bitcast.18, () %tuple.35, (s32[1,2]{1,0:T(1,128)S(1)}, f32[2,1024,1024]{2,1,0:T(8,128)}, f32[16,256,1024]{2,1,0:T(8,128)}) %tuple.36), branch_computations={%region_1.1_spmd, %region_2.2_spmd} | conditional | flops 3221225472 | bytes 6292042 | solution.py:23
  446.6 8.5 %conditional.2 = (f32[1,1024,256]{2,1,0:T(8,128)S(1)}) conditional(s32[]{:T(128)} %bitcast.18, () %tuple.35, (s32[1,2]{1,0:T(1,128)S(1)}, f32[2,1024,1024]{2,1,0:T(8,128)}, f32[16,256,1024]{2,1,0:T(8,128)}) %tuple.36), branch_computations={%region_1.1_spmd, %region_2.2_spmd} | conditional | flops 3221225472 | bytes 6292042 | solution.py:23
  457.3 8.6 %conditional.2 = (f32[1,1024,256]{2,1,0:T(8,128)S(1)}) conditional(s32[]{:T(128)} %bitcast.18, () %tuple.35, (s32[1,2]{1,0:T(1,128)S(1)}, f32[2,1024,1024]{2,1,0:T(8,128)}, f32[16,256,1024]{2,1,0:T(8,128)}) %tuple.36), branch_computations={%region_1.1_spmd, %region_2.2_spmd} | conditional | flops 3221225472 | bytes 6292042 | solution.py:23
  460.3 5.6 %fusion.3 = f32[1,1024,256]{2,1,0:T(8,128)S(1)} fusion(f32[2,1024,1024]{2,1,0:T(8,128)} %get-tuple-element.31, s32[]{:T(128)S(6)} %select_n.0, f32[16,256,1024]{2,1,0:T(8,128)} %get-tuple-element.33, s32[]{:T(128)} %bitcast.2), kind=kOutput, calls=%fused_computation.3 | convolution fusion | flops 3221225472 | bytes 6291972 | tf_op jit(solution)/shard_map/while/body/eval_jaxpr/cond/branch_1_fun/ak,bk->ab/dot_general | solution.py:10
  468.1 8.5 %conditional.2 = (f32[1,1024,256]{2,1,0:T(8,128)S(1)}) conditional(s32[]{:T(128)} %bitcast.18, () %tuple.35, (s32[1,2]{1,0:T(1,128)S(1)}, f32[2,1024,1024]{2,1,0:T(8,128)}, f32[16,256,1024]{2,1,0:T(8,128)}) %tuple.36), branch_computations={%region_1.1_spmd, %region_2.2_spmd} | conditional | flops 3221225472 | bytes 6292042 | solution.py:23
  478.9 8.6 %conditional.2 = (f32[1,1024,256]{2,1,0:T(8,128)S(1)}) conditional(s32[]{:T(128)} %bitcast.18, () %tuple.35, (s32[1,2]{1,0:T(1,128)S(1)}, f32[2,1024,1024]{2,1,0:T(8,128)}, f32[16,256,1024]{2,1,0:T(8,128)}) %tuple.36), branch_computations={%region_1.1_spmd, %region_2.2_spmd} | conditional | flops 3221225472 | bytes 6292042 | solution.py:23
  489.6 8.5 %conditional.2 = (f32[1,1024,256]{2,1,0:T(8,128)S(1)}) conditional(s32[]{:T(128)} %bitcast.18, () %tuple.35, (s32[1,2]{1,0:T(1,128)S(1)}, f32[2,1024,1024]{2,1,0:T(8,128)}, f32[16,256,1024]{2,1,0:T(8,128)}) %tuple.36), branch_computations={%region_1.1_spmd, %region_2.2_spmd} | conditional | flops 3221225472 | bytes 6292042 | solution.py:23
  500.4 8.6 %conditional.2 = (f32[1,1024,256]{2,1,0:T(8,128)S(1)}) conditional(s32[]{:T(128)} %bitcast.18, () %tuple.35, (s32[1,2]{1,0:T(1,128)S(1)}, f32[2,1024,1024]{2,1,0:T(8,128)}, f32[16,256,1024]{2,1,0:T(8,128)}) %tuple.36), branch_computations={%region_1.1_spmd, %region_2.2_spmd} | conditional | flops 3221225472 | bytes 6292042 | solution.py:23
  503.3 5.6 %fusion.3 = f32[1,1024,256]{2,1,0:T(8,128)S(1)} fusion(f32[2,1024,1024]{2,1,0:T(8,128)} %get-tuple-element.31, s32[]{:T(128)S(6)} %select_n.0, f32[16,256,1024]{2,1,0:T(8,128)} %get-tuple-element.33, s32[]{:T(128)} %bitcast.2), kind=kOutput, calls=%fused_computation.3 | convolution fusion | flops 3221225472 | bytes 6291972 | tf_op jit(solution)/shard_map/while/body/eval_jaxpr/cond/branch_1_fun/ak,bk->ab/dot_general | solution.py:10
  511.1 8.5 %conditional.2 = (f32[1,1024,256]{2,1,0:T(8,128)S(1)}) conditional(s32[]{:T(128)} %bitcast.18, () %tuple.35, (s32[1,2]{1,0:T(1,128)S(1)}, f32[2,1024,1024]{2,1,0:T(8,128)}, f32[16,256,1024]{2,1,0:T(8,128)}) %tuple.36), branch_computations={%region_1.1_spmd, %region_2.2_spmd} | conditional | flops 3221225472 | bytes 6292042 | solution.py:23
  520.7 21.9 %sub.3 = f32[20,1024,256]{2,1,0:T(8,128)} subtract(f32[20,1024,256]{2,1,0:T(8,128)} %param.10, f32[20,1024,256]{2,1,0:T(8,128)} %get-tuple-element.43) | non-fusion elementwise | flops 5242880 | bytes 62914560 | tf_op jit(solution)/shard_map/sub | solution.py:30
  (108 shorter events, 124.3 us)
Async XLA Ops:
  7.2 49.6 %copy-start = (f32[2,256,1024]{2,1,0:T(8,128)S(1)}, f32[2,256,1024]{2,1,0:T(8,128)}, u32[]{:S(2)}) copy-start(f32[2,256,1024]{2,1,0:T(8,128)} %param.9) | copy-start | bytes 6291460
  7.2 60.0 %copy-start.2 = (s32[20,2]{0,1:T(2,128)S(1)}, s32[20,2]{0,1:T(2,128)}, u32[]{:S(2)}) copy-start(s32[20,2]{0,1:T(2,128)} %param.11) | copy-start | bytes 484
  7.2 49.6 %all-gather.4.cloned.1.call-start = ((), (), s32[]{:S(2)}) async-start(), calls=%async_computation | async-start | bytes 4718592 | tf_op jit(solution)/shard_map/all_gather | solution.py:14
  7.9 145.6 %all-gather.6.cloned.1.call-start = ((), (), s32[]{:S(2)}) async-start(), calls=%async_computation.1 | async-start | bytes 10485760 | tf_op jit(solution)/shard_map/all_gather | solution.py:18
  66.4 239.1 %all-gather.8.cloned.1.call-start = ((), (), s32[]{:S(2)}) async-start(), calls=%async_computation.2 | async-start | bytes 18874368 | tf_op jit(solution)/shard_map/all_gather | solution.py:19
  520.7 21.9 %copy-start.1 = (f32[2,256,1024]{2,1,0:T(8,128)S(1)}, f32[2,256,1024]{2,1,0:T(8,128)}, u32[]{:S(2)}) copy-start(f32[2,256,1024]{2,1,0:T(8,128)} %param.9) | copy-start | bytes 6291460
Sparse Core Ops, SparseCore 0:
  9.6 47.1 all-gather.3
  66.6 86.8 all-gather.5
  155.7 149.8 all-gather.7
where the time goes:
time: 550 us; the launch traced here: 549 us
  waiting for transfers between devices  288 us (52%)
  matrix products  121 us (22%)
  loops' own time  59 us (11%)
  local copies, waits for them, and re-layouts  44.7 us (8%)
  other arithmetic  21.9 us (4%)
  between operations  13.8 us (3%)
    all_gather x1, waiting for transfers between devices, per_device(): slices = lax.all_gather(solved, 'row', axis=0, tiled=True)  152 us
    dot_general x20, matrix products, slot_term(): return jnp.einsum('ak,bk->ab', left_tile, right_rows, precision=highest)  112 us
    all_gather x1, waiting for transfers between devices, per_device(): whole_tiles = lax.all_gather(solved, 'col', axis=1, tiled=True)  86.2 us
    all_gather x1, waiting for transfers between devices, per_device(): full_pivot = lax.all_gather(pivot_inverse, 'row', axis=0, tiled=True)  48.8 us
    another operation x20, loops' own time, owner_slot(): lax.cond(listed[1] >= 0, lambda: slot_term(whole_tiles[listed[0]], slices...  47.3 us
    sub x1, other arithmetic, per_device(): return (solved, trailing - updates)  21.9 us
    dynamic_update_slice x20, local copies, waits for them, and re-layouts, per_device(): updates = lax.map(owner_slot, tile_list)  20.9 us
    slice x20, local copies, waits for them, and re-layouts, owner_slot(): listed[1]  12.1 us
  transfers between devices with their start and end apart: 3, of which 3 were waited for; matrix products, arithmetic and copies ran while one was open for 0% of the time, Pallas kernels for 0%

commit v1 on v0

--- a/solution.py
+++ b/solution.py
@@ -1,9 +1,38 @@
+import functools
 import jax
 import jax.numpy as jnp
 from jax import lax
 from jax.sharding import PartitionSpec as P
 
 highest = lax.Precision.HIGHEST
+
+
+def _assign_points(packet, d0):
+    state_next = list(packet.shape[1:])
+    state_next[d0] *= packet.shape[0]
+    return jnp.moveaxis(packet, 0, d0).reshape(state_next)
+
+
+def apply_stops_all_by_axis(incoming_x, link_axis):
+    p_next, local_part = (jax.lax.axis_size(link_axis), jax.lax.axis_index(link_axis))
+    x_next, v_now = (incoming_x[None], 1)
+    while v_now < p_next:
+        block_last = jax.lax.ppermute(
+            x_next, axis_name=link_axis, perm=tuple(((i, i ^ v_now) for i in range(p_next)))
+        )
+        seen_now = local_part & v_now == 0
+        x_next = jnp.concatenate(
+            [jnp.where(seen_now, x_next, block_last), jnp.where(seen_now, block_last, x_next)]
+        )
+        v_now *= 2
+    return x_next
+
+
+def fit_the_results(target, obj, k_dim):
+    return _assign_points(apply_stops_all_by_axis(target, obj), k_dim)
+
+
+take_tails_by_axis = functools.partial(fit_the_results, obj="col", k_dim=1)
 
 
 def slot_term(left_tile, right_rows):
@@ -15,7 +44,7 @@
     slice_rows = panel.shape[1]
     tile_order = panel.shape[2]
     solved = jnp.einsum("pak,jk->paj", panel, full_pivot, precision=highest)
-    whole_tiles = lax.all_gather(solved, "col", axis=1, tiled=True)
+    whole_tiles = take_tails_by_axis(solved)
     slices = lax.all_gather(solved, "row", axis=0, tiled=True)
     empty_term = jnp.zeros((tile_order, slice_rows), jnp.float32)
 

time: 550 us -> 475 us (0.86)
  waiting for transfers between devices: 288 us -> 186 us
  other arithmetic: 21.9 us -> 39.8 us
    all_gather x1, waiting for transfers between devices: 152 us -> 0.01 us  [per_device(): slices = lax.all_gather(solved, 'row', axis=0, tiled=True)]
    ppermute x0 -> x2, waiting for transfers between devices: none -> 136 us  [apply_stops_all_by_axis(): jax.lax.ppermute(x_next, axis_name=link_axis, perm=tuple(((i, i ^ v_now)...]
    all_gather x1 -> x0, waiting for transfers between devices: 86.2 us -> none  [per_device(): whole_tiles = lax.all_gather(solved, 'col', axis=1, tiled=True)]
    select_n x0 -> x2, other arithmetic: none -> 11 us  [apply_stops_all_by_axis(): jnp.where(seen_now, x_next, block_last)]
  transfers between devices with their start and end apart: 3 -> 4, of which waited for: 3 -> 3; matrix products, arithmetic and copies ran while one was open for 0% -> 5% of each run, Pallas kernels for 0% -> 0%
where the time goes in v1:
time: 475 us; the launch traced here: 473 us
  waiting for transfers between devices  186 us (39%)
  matrix products  121 us (25%)
  loops' own time  61.7 us (13%)
  local copies, waits for them, and re-layouts  48.1 us (10%)
  other arithmetic  39.8 us (8%)
  between operations  14.1 us (3%)
    ppermute x2, waiting for transfers between devices, apply_stops_all_by_axis(): jax.lax.ppermute(x_next, axis_name=link_axis, perm=tuple(((i, i ^ v_now)...  136 us
    dot_general x20, matrix products, slot_term(): return jnp.einsum('ak,bk->ab', left_tile, right_rows, precision=highest)  112 us
    another operation x20, loops' own time, owner_slot(): lax.cond(listed[1] >= 0, lambda: slot_term(whole_tiles[listed[0]], slices...  50.1 us
    all_gather x1, waiting for transfers between devices, per_device(): full_pivot = lax.all_gather(pivot_inverse, 'row', axis=0, tiled=True)  48.8 us
    sub x1, other arithmetic, per_device(): return (solved, trailing - updates)  21.9 us
    dynamic_update_slice x20, local copies, waits for them, and re-layouts, per_device(): updates = lax.map(owner_slot, tile_list)  20.9 us
    slice x20, local copies, waits for them, and re-layouts, owner_slot(): listed[1]  11.8 us
    another operation x1, loops' own time, per_device(): updates = lax.map(owner_slot, tile_list)  11.7 us
  transfers between devices with their start and end apart: 4, of which 3 were waited for; matrix products, arithmetic and copies ran while one was open for 5% of the time, Pallas kernels for 0%

profile of v1, /device:TPU:17, one launch (start us, length us, event | category | flops | bytes accessed | tf_op | source)
XLA Modules:
  0.0 473.1 jit_solution(14836523222175139621)
XLA Ops:
  8.0 48.8 %all-gather.3.cloned.1.call-done = f32[1024,1024]{1,0:T(8,128)} async-done(((f32[128,1024]{1,0:T(8,128)}), f32[1024,1024]{1,0:T(8,128)}) %all-gather.3.cloned.1.call-update) | async-done | bytes 4194320 | tf_op jit(solution)/shard_map/all_gather | solution.py:43
  56.8 9.6 %fusion.9 = f32[2,256,1024]{2,1,0:T(8,128)} fusion(f32[2,256,1024]{2,1,0:T(8,128)S(1)} %copy-done, f32[1024,1024]{1,0:T(8,128)} %all-gather.3.cloned.1.call-done), kind=kOutput, calls=%fused_computation.11 | convolution fusion | flops 6442450944 | bytes 8388608 | tf_op jit(solution)/shard_map/pak,jk->paj/dot_general | solution.py:46
  67.7 46.0 %collective-permute-done = f32[1,2,256,1024]{3,2,1,0:T(8,128)} collective-permute-done((f32[1,2,256,1024]{3,2,1,0:T(8,128)}, f32[1,2,256,1024]{3,2,1,0:T(8,128)}, u32[]{:S(2)}, u32[]{:S(2)}) %collective-permute-start) | collective-permute-done | bytes 2097184 | tf_op jit(solution)/shard_map/ppermute | solution.py:20
  120.6 90.0 %collective-permute-done.1 = f32[2,2,256,1024]{3,2,1,0:T(8,128)} collective-permute-done((f32[2,2,256,1024]{3,2,1,0:T(8,128)}, f32[2,2,256,1024]{3,2,1,0:T(8,128)}, u32[]{:S(2)}, u32[]{:S(2)}) %collective-permute-start.1) | collective-permute-done | bytes 4194336 | tf_op jit(solution)/shard_map/ppermute | solution.py:20
  210.6 8.1 %broadcast_select_fusion.1 = (f32[2,2,256,1024]{3,2,1,0:T(8,128)}, f32[2,2,256,1024]{3,2,1,0:T(8,128)}) fusion(f32[2,2,256,1024]{3,2,1,0:T(8,128)} %collective-permute-done.1, pred[]{:T(512)S(6)} %eq.6, f32[1,2,256,1024]{3,2,1,0:T(8,128)} %copy-done.2, f32[1,2,256,1024]{3,2,1,0:T(8,128)S(1)} %get-tuple-element.73), kind=kLoop, calls=%fused_computation.14 | loop fusion | flops 3145728 | bytes 16777216 | tf_op jit(solution)/shard_map/jit(_where)/select_n | solution.py:25
  227.1 217.2 %while.10 = (s32[]{:T(128)}, f32[20,1024,256]{2,1,0:T(8,128)}, s32[20,2]{1,0:T(8,128)S(1)}, f32[2,1024,1024]{2,1,0:T(8,128)}, f32[16,256,1024]{2,1,0:T(8,128)}, /*index=5*/s32[]{:T(128)}, s32[1,1]{1,0:T(1,128)}) while((s32[]{:T(128)}, f32[20,1024,256]{2,1,0:T(8,128)}, s32[20,2]{1,0:T(8,128)S(1)}, f32[2,1024,1024]{2,1,0:T(8,128)}, ...), condition=%wide.region_3.4_spmd, body=%wide.region_0.3_spmd.sunk | while | flops 3221225472 | bytes 8389849 | solution.py:58
  228.2 8.7 %conditional.2 = (f32[1,1024,256]{2,1,0:T(8,128)S(1)}) conditional(s32[]{:T(128)} %bitcast.24, () %tuple.38, (s32[1,2]{1,0:T(1,128)S(1)}, f32[2,1024,1024]{2,1,0:T(8,128)}, f32[16,256,1024]{2,1,0:T(8,128)}) %tuple.39), branch_computations={%region_1.1_spmd, %region_2.2_spmd} | conditional | flops 3221225472 | bytes 6292042 | solution.py:52
  239.1 8.7 %conditional.2 = (f32[1,1024,256]{2,1,0:T(8,128)S(1)}) conditional(s32[]{:T(128)} %bitcast.24, () %tuple.38, (s32[1,2]{1,0:T(1,128)S(1)}, f32[2,1024,1024]{2,1,0:T(8,128)}, f32[16,256,1024]{2,1,0:T(8,128)}) %tuple.39), branch_computations={%region_1.1_spmd, %region_2.2_spmd} | conditional | flops 3221225472 | bytes 6292042 | solution.py:52
  249.9 8.7 %conditional.2 = (f32[1,1024,256]{2,1,0:T(8,128)S(1)}) conditional(s32[]{:T(128)} %bitcast.24, () %tuple.38, (s32[1,2]{1,0:T(1,128)S(1)}, f32[2,1024,1024]{2,1,0:T(8,128)}, f32[16,256,1024]{2,1,0:T(8,128)}) %tuple.39), branch_computations={%region_1.1_spmd, %region_2.2_spmd} | conditional | flops 3221225472 | bytes 6292042 | solution.py:52
  260.8 8.7 %conditional.2 = (f32[1,1024,256]{2,1,0:T(8,128)S(1)}) conditional(s32[]{:T(128)} %bitcast.24, () %tuple.38, (s32[1,2]{1,0:T(1,128)S(1)}, f32[2,1024,1024]{2,1,0:T(8,128)}, f32[16,256,1024]{2,1,0:T(8,128)}) %tuple.39), branch_computations={%region_1.1_spmd, %region_2.2_spmd} | conditional | flops 3221225472 | bytes 6292042 | solution.py:52
  271.6 8.7 %conditional.2 = (f32[1,1024,256]{2,1,0:T(8,128)S(1)}) conditional(s32[]{:T(128)} %bitcast.24, () %tuple.38, (s32[1,2]{1,0:T(1,128)S(1)}, f32[2,1024,1024]{2,1,0:T(8,128)}, f32[16,256,1024]{2,1,0:T(8,128)}) %tuple.39), branch_computations={%region_1.1_spmd, %region_2.2_spmd} | conditional | flops 3221225472 | bytes 6292042 | solution.py:52
  274.7 5.6 %fusion.3 = f32[1,1024,256]{2,1,0:T(8,128)S(1)} fusion(f32[2,1024,1024]{2,1,0:T(8,128)} %get-tuple-element.31, s32[]{:T(128)S(6)} %select_n.21, f32[16,256,1024]{2,1,0:T(8,128)} %get-tuple-element.33, s32[]{:T(128)} %bitcast.2), kind=kOutput, calls=%fused_computation.3 | convolution fusion | flops 3221225472 | bytes 6291972 | tf_op jit(solution)/shard_map/while/body/eval_jaxpr/cond/branch_1_fun/ak,bk->ab/dot_general | solution.py:39
  282.5 8.7 %conditional.2 = (f32[1,1024,256]{2,1,0:T(8,128)S(1)}) conditional(s32[]{:T(128)} %bitcast.24, () %tuple.38, (s32[1,2]{1,0:T(1,128)S(1)}, f32[2,1024,1024]{2,1,0:T(8,128)}, f32[16,256,1024]{2,1,0:T(8,128)}) %tuple.39), branch_computations={%region_1.1_spmd, %region_2.2_spmd} | conditional | flops 3221225472 | bytes 6292042 | solution.py:52
  293.4 8.7 %conditional.2 = (f32[1,1024,256]{2,1,0:T(8,128)S(1)}) conditional(s32[]{:T(128)} %bitcast.24, () %tuple.38, (s32[1,2]{1,0:T(1,128)S(1)}, f32[2,1024,1024]{2,1,0:T(8,128)}, f32[16,256,1024]{2,1,0:T(8,128)}) %tuple.39), branch_computations={%region_1.1_spmd, %region_2.2_spmd} | conditional | flops 3221225472 | bytes 6292042 | solution.py:52
  304.2 8.7 %conditional.2 = (f32[1,1024,256]{2,1,0:T(8,128)S(1)}) conditional(s32[]{:T(128)} %bitcast.24, () %tuple.38, (s32[1,2]{1,0:T(1,128)S(1)}, f32[2,1024,1024]{2,1,0:T(8,128)}, f32[16,256,1024]{2,1,0:T(8,128)}) %tuple.39), branch_computations={%region_1.1_spmd, %region_2.2_spmd} | conditional | flops 3221225472 | bytes 6292042 | solution.py:52
  307.3 5.6 %fusion.3 = f32[1,1024,256]{2,1,0:T(8,128)S(1)} fusion(f32[2,1024,1024]{2,1,0:T(8,128)} %get-tuple-element.31, s32[]{:T(128)S(6)} %select_n.21, f32[16,256,1024]{2,1,0:T(8,128)} %get-tuple-element.33, s32[]{:T(128)} %bitcast.2), kind=kOutput, calls=%fused_computation.3 | convolution fusion | flops 3221225472 | bytes 6291972 | tf_op jit(solution)/shard_map/while/body/eval_jaxpr/cond/branch_1_fun/ak,bk->ab/dot_general | solution.py:39
  315.1 8.7 %conditional.2 = (f32[1,1024,256]{2,1,0:T(8,128)S(1)}) conditional(s32[]{:T(128)} %bitcast.24, () %tuple.38, (s32[1,2]{1,0:T(1,128)S(1)}, f32[2,1024,1024]{2,1,0:T(8,128)}, f32[16,256,1024]{2,1,0:T(8,128)}) %tuple.39), branch_computations={%region_1.1_spmd, %region_2.2_spmd} | conditional | flops 3221225472 | bytes 6292042 | solution.py:52
  326.0 8.7 %conditional.2 = (f32[1,1024,256]{2,1,0:T(8,128)S(1)}) conditional(s32[]{:T(128)} %bitcast.24, () %tuple.38, (s32[1,2]{1,0:T(1,128)S(1)}, f32[2,1024,1024]{2,1,0:T(8,128)}, f32[16,256,1024]{2,1,0:T(8,128)}) %tuple.39), branch_computations={%region_1.1_spmd, %region_2.2_spmd} | conditional | flops 3221225472 | bytes 6292042 | solution.py:52
  336.8 8.7 %conditional.2 = (f32[1,1024,256]{2,1,0:T(8,128)S(1)}) conditional(s32[]{:T(128)} %bitcast.24, () %tuple.38, (s32[1,2]{1,0:T(1,128)S(1)}, f32[2,1024,1024]{2,1,0:T(8,128)}, f32[16,256,1024]{2,1,0:T(8,128)}) %tuple.39), branch_computations={%region_1.1_spmd, %region_2.2_spmd} | conditional | flops 3221225472 | bytes 6292042 | solution.py:52
  347.7 8.7 %conditional.2 = (f32[1,1024,256]{2,1,0:T(8,128)S(1)}) conditional(s32[]{:T(128)} %bitcast.24, () %tuple.38, (s32[1,2]{1,0:T(1,128)S(1)}, f32[2,1024,1024]{2,1,0:T(8,128)}, f32[16,256,1024]{2,1,0:T(8,128)}) %tuple.39), branch_computations={%region_1.1_spmd, %region_2.2_spmd} | conditional | flops 3221225472 | bytes 6292042 | solution.py:52
  358.5 8.7 %conditional.2 = (f32[1,1024,256]{2,1,0:T(8,128)S(1)}) conditional(s32[]{:T(128)} %bitcast.24, () %tuple.38, (s32[1,2]{1,0:T(1,128)S(1)}, f32[2,1024,1024]{2,1,0:T(8,128)}, f32[16,256,1024]{2,1,0:T(8,128)}) %tuple.39), branch_computations={%region_1.1_spmd, %region_2.2_spmd} | conditional | flops 3221225472 | bytes 6292042 | solution.py:52
  369.4 8.7 %conditional.2 = (f32[1,1024,256]{2,1,0:T(8,128)S(1)}) conditional(s32[]{:T(128)} %bitcast.24, () %tuple.38, (s32[1,2]{1,0:T(1,128)S(1)}, f32[2,1024,1024]{2,1,0:T(8,128)}, f32[16,256,1024]{2,1,0:T(8,128)}) %tuple.39), branch_computations={%region_1.1_spmd, %region_2.2_spmd} | conditional | flops 3221225472 | bytes 6292042 | solution.py:52
  372.5 5.6 %fusion.3 = f32[1,1024,256]{2,1,0:T(8,128)S(1)} fusion(f32[2,1024,1024]{2,1,0:T(8,128)} %get-tuple-element.31, s32[]{:T(128)S(6)} %select_n.21, f32[16,256,1024]{2,1,0:T(8,128)} %get-tuple-element.33, s32[]{:T(128)} %bitcast.2), kind=kOutput, calls=%fused_computation.3 | convolution fusion | flops 3221225472 | bytes 6291972 | tf_op jit(solution)/shard_map/while/body/eval_jaxpr/cond/branch_1_fun/ak,bk->ab/dot_general | solution.py:39
  380.3 8.7 %conditional.2 = (f32[1,1024,256]{2,1,0:T(8,128)S(1)}) conditional(s32[]{:T(128)} %bitcast.24, () %tuple.38, (s32[1,2]{1,0:T(1,128)S(1)}, f32[2,1024,1024]{2,1,0:T(8,128)}, f32[16,256,1024]{2,1,0:T(8,128)}) %tuple.39), branch_computations={%region_1.1_spmd, %region_2.2_spmd} | conditional | flops 3221225472 | bytes 6292042 | solution.py:52
  391.1 8.7 %conditional.2 = (f32[1,1024,256]{2,1,0:T(8,128)S(1)}) conditional(s32[]{:T(128)} %bitcast.24, () %tuple.38, (s32[1,2]{1,0:T(1,128)S(1)}, f32[2,1024,1024]{2,1,0:T(8,128)}, f32[16,256,1024]{2,1,0:T(8,128)}) %tuple.39), branch_computations={%region_1.1_spmd, %region_2.2_spmd} | conditional | flops 3221225472 | bytes 6292042 | solution.py:52
  402.0 8.7 %conditional.2 = (f32[1,1024,256]{2,1,0:T(8,128)S(1)}) conditional(s32[]{:T(128)} %bitcast.24, () %tuple.38, (s32[1,2]{1,0:T(1,128)S(1)}, f32[2,1024,1024]{2,1,0:T(8,128)}, f32[16,256,1024]{2,1,0:T(8,128)}) %tuple.39), branch_computations={%region_1.1_spmd, %region_2.2_spmd} | conditional | flops 3221225472 | bytes 6292042 | solution.py:52
  405.1 5.6 %fusion.3 = f32[1,1024,256]{2,1,0:T(8,128)S(1)} fusion(f32[2,1024,1024]{2,1,0:T(8,128)} %get-tuple-element.31, s32[]{:T(128)S(6)} %select_n.21, f32[16,256,1024]{2,1,0:T(8,128)} %get-tuple-element.33, s32[]{:T(128)} %bitcast.2), kind=kOutput, calls=%fused_computation.3 | convolution fusion | flops 3221225472 | bytes 6291972 | tf_op jit(solution)/shard_map/while/body/eval_jaxpr/cond/branch_1_fun/ak,bk->ab/dot_general | solution.py:39
  412.8 8.7 %conditional.2 = (f32[1,1024,256]{2,1,0:T(8,128)S(1)}) conditional(s32[]{:T(128)} %bitcast.24, () %tuple.38, (s32[1,2]{1,0:T(1,128)S(1)}, f32[2,1024,1024]{2,1,0:T(8,128)}, f32[16,256,1024]{2,1,0:T(8,128)}) %tuple.39), branch_computations={%region_1.1_spmd, %region_2.2_spmd} | conditional | flops 3221225472 | bytes 6292042 | solution.py:52
  423.7 8.7 %conditional.2 = (f32[1,1024,256]{2,1,0:T(8,128)S(1)}) conditional(s32[]{:T(128)} %bitcast.24, () %tuple.38, (s32[1,2]{1,0:T(1,128)S(1)}, f32[2,1024,1024]{2,1,0:T(8,128)}, f32[16,256,1024]{2,1,0:T(8,128)}) %tuple.39), branch_computations={%region_1.1_spmd, %region_2.2_spmd} | conditional | flops 3221225472 | bytes 6292042 | solution.py:52
  434.6 8.7 %conditional.2 = (f32[1,1024,256]{2,1,0:T(8,128)S(1)}) conditional(s32[]{:T(128)} %bitcast.24, () %tuple.38, (s32[1,2]{1,0:T(1,128)S(1)}, f32[2,1024,1024]{2,1,0:T(8,128)}, f32[16,256,1024]{2,1,0:T(8,128)}) %tuple.39), branch_computations={%region_1.1_spmd, %region_2.2_spmd} | conditional | flops 3221225472 | bytes 6292042 | solution.py:52
  437.6 5.6 %fusion.3 = f32[1,1024,256]{2,1,0:T(8,128)S(1)} fusion(f32[2,1024,1024]{2,1,0:T(8,128)} %get-tuple-element.31, s32[]{:T(128)S(6)} %select_n.21, f32[16,256,1024]{2,1,0:T(8,128)} %get-tuple-element.33, s32[]{:T(128)} %bitcast.2), kind=kOutput, calls=%fused_computation.3 | convolution fusion | flops 3221225472 | bytes 6291972 | tf_op jit(solution)/shard_map/while/body/eval_jaxpr/cond/branch_1_fun/ak,bk->ab/dot_general | solution.py:39
  444.3 21.9 %sub.3 = f32[20,1024,256]{2,1,0:T(8,128)} subtract(f32[20,1024,256]{2,1,0:T(8,128)} %param.10, f32[20,1024,256]{2,1,0:T(8,128)} %get-tuple-element.43) | non-fusion elementwise | flops 5242880 | bytes 62914560 | tf_op jit(solution)/shard_map/sub | solution.py:59
  (116 shorter events, 144.8 us)
Async XLA Ops:
  7.2 49.6 %copy-start = (f32[2,256,1024]{2,1,0:T(8,128)S(1)}, f32[2,256,1024]{2,1,0:T(8,128)}, u32[]{:S(2)}) copy-start(f32[2,256,1024]{2,1,0:T(8,128)} %param.9) | copy-start | bytes 6291460
  7.2 49.6 %all-gather.3.cloned.1.call-start = ((), (), s32[]{:S(2)}) async-start(), calls=%async_computation | async-start | bytes 4718592 | tf_op jit(solution)/shard_map/all_gather | solution.py:43
  7.9 219.2 %all-gather.5.cloned.1.call-start = ((), (), s32[]{:S(2)}) async-start(), calls=%async_computation.1 | async-start | bytes 18874368 | tf_op jit(solution)/shard_map/all_gather | solution.py:48
  66.4 47.3 %collective-permute-start = (f32[1,2,256,1024]{3,2,1,0:T(8,128)}, f32[1,2,256,1024]{3,2,1,0:T(8,128)}, u32[]{:S(2)}, u32[]{:S(2)}) collective-permute-start(f32[1,2,256,1024]{3,2,1,0:T(8,128)} %bitcast.26), channel_id=1, source_target_pairs={{0,1},{1,0},{2,3},{3,2},{4,5},{5,4},{6,7},{7,6},{8,9},{9,8},{10,11... | collective-permute-start | bytes 6291464 | tf_op jit(solution)/shard_map/ppermute | solution.py:20
  116.6 2.7 copy-start.2
  116.6 3.9 copy-start.3
  119.3 91.3 %collective-permute-start.1 = (f32[2,2,256,1024]{3,2,1,0:T(8,128)}, f32[2,2,256,1024]{3,2,1,0:T(8,128)}, u32[]{:S(2)}, u32[]{:S(2)}) collective-permute-start(f32[2,2,256,1024]{3,2,1,0:T(8,128)} %pad_maximum_fusion), channel_id=1, source_target_pairs={{0,2},{1,3},{2,0},{3,1},{4,6},{5,7},{6,4},{7,5},{8,10},{9,11},{10,... | collective-permute-start | bytes 12582920 | tf_op jit(solution)/shard_map/ppermute | solution.py:20
  444.3 21.9 %copy-start.1 = (f32[2,256,1024]{2,1,0:T(8,128)S(1)}, f32[2,256,1024]{2,1,0:T(8,128)}, u32[]{:S(2)}) copy-start(f32[2,256,1024]{2,1,0:T(8,128)} %param.9) | copy-start | bytes 6291460
Sparse Core Ops, SparseCore 0:
  9.6 47.1 all-gather.2
  66.6 149.2 all-gather.4
